TPU v7x, 128 devices: a whole 4x4x4 slice. The times are simulated.
128 devices in a mesh: gz: 32 (over y, z, core), phi: 4 (over x).
Axes of the slice: x: 4, y: 4, z: 4, core: 2. Of those that a mesh axis runs over, the one named last changes fastest.
Arguments:
- field: float32 [16, 4, 2048, 1024], P(None, None, 'gz', 'phi'), may hold values from -6 to 6
- field_tangent: float32 [16, 4, 2048, 1024], P(None, None, 'gz', 'phi'), may hold values from -6 to 6
- spectral_weight: float32 [2, 16, 16, 64, 64], P(None, None, None, 'gz', 'phi'), may hold values from -1 to 1
- local_weight: float32 [16, 16], replicated, may hold values from -1.5 to 1.5
- bias_term: float32 [16], replicated, may hold values from -3 to 3
- z_modes: int32 [64], replicated, may hold values from 0 to 1023, as said below
- phi_modes: int32 [64], replicated, may hold values from 0 to 1023, as said below
Outputs:
- output: float32 [16, 4, 2048, 1024], P(None, None, 'gz', 'phi')
- output_tangent: float32 [16, 4, 2048, 1024], P(None, None, 'gz', 'phi')
Inputs may be any that keep to these rules, and one draw needn't show every extreme that they name: `z_modes`: entries may repeat; 0 and 1023 both occur. `phi_modes`: entries may repeat; 0 and 1023 both occur.
All inputs are finite; a program needn't handle non-finite values.
Results may differ from a plain program's by a relative error of at most 0.000078.
Values sent between devices are 32-bit elements; how exact they have to be, the bound alone decides.
A program may use at most 128 MiB of HBM per device.

v0:
```python
import functools
import math

import jax
import jax.numpy as jnp
from jax import lax
from jax.experimental import pallas as pl
from jax.experimental.pallas import tpu as pltpu
from jax.sharding import PartitionSpec as P

C, R, ZL, FL = 16, 4, 64, 256
Z, PHI, KZ, KP = 2048, 1024, 64, 64
F32, BF16, I32 = jnp.float32, jnp.bfloat16, jnp.int32
MESH = pl.DeviceIdType.MESH
VMEM_FORWARD = 48 << 20
VMEM_EXCHANGE = 24 << 20
VMEM_INVERSE = 24 << 20
SCALE = (1.0 / math.sqrt(Z * PHI)) * (2.0 / math.sqrt(KZ * KP))


def iota(shape, dim):
    return lax.broadcasted_iota(I32, shape, dim)


def split(x):
    hi = x.astype(BF16)
    return hi, (x - hi.astype(F32)).astype(BF16)


def wave(turns, length):
    quarter = length // 4
    near = ((turns + 2 * quarter) & (length - 1)) - 2 * quarter
    x = (quarter - jnp.abs(near)).astype(F32) * (2.0 * math.pi / length)
    x2 = x * x
    acc = 1.0 / math.factorial(13)
    for n in (11, 9, 7, 5, 3, 1):
        acc = acc * x2 + (1.0 if n % 4 == 1 else -1.0) / math.factorial(n)
    return acc * x


def nt(a, b):
    return lax.dot_general(a, b, (((1,), (1,)), ((), ())), preferred_element_type=F32)


def nn(a, b):
    return jnp.dot(a, b, preferred_element_type=F32)


def pick_column(modes_ref, which):
    hit = iota((128, 64), 1) == which
    return jnp.sum(jnp.where(hit, modes_ref[...].astype(F32), 0.0), axis=1, keepdims=True).astype(I32)


def phi_table(modes_ref):
    row = iota((128, 64), 0)
    col = pick_column(modes_ref, row // 16 * 8 + row % 8)
    f = lax.axis_index("phi") * FL + iota((128, FL), 1)
    return wave(f * col + (iota((128, FL), 0) // 8 % 2) * (PHI // 4), PHI)


def z_table(modes_ref, z, turn):
    row = iota((128, 64), 0)
    col = pick_column(modes_ref, row // 4 % 16 * 4 + row // 64 * 2 + row // 2 % 2)
    return wave((lax.axis_index("gz") * ZL + z) * col + turn, Z)


def places(j):
    q = 2 * j
    base = ((q // 16) * 1024 + (q // 8 % 2) * 128 + q % 8, (q // 8) * 128 + q % 8 + 4096)
    step = (256, 1024)
    return [
        [pl.ds(base[g // 8] + (n + (g % 8 // 2) * step[g // 8] + (g % 2) * 64), 8, stride=8) for g in range(16)]
        for n in range(2)
    ]


def fetch(x0_ref, x1_ref, x_buf, sem, zb):
    copies = []
    for p, src in enumerate((x0_ref, x1_ref)):
        for h in range(2):
            n = zb * 4 + p * 2 + h
            copies.append(pltpu.make_async_copy(
                src.at[:, pl.ds(pl.multiple_of(zb * 8, 8), 8), pl.ds(h * 128, 128)], x_buf.at[n], sem.at[n]
            ))
    return copies


def stack_z(x_buf, zb, i):
    flat = x_buf.reshape(32 * 512, 128)
    a, b, c, d = (flat[pl.ds(zb * 2048 + n * 512 + i, 64, stride=8), :] for n in range(4))
    return jnp.concatenate([jnp.concatenate([a, b], axis=1), jnp.concatenate([c, d], axis=1)], axis=0)


def cat(parts, axis):
    return jnp.concatenate(parts, axis=axis)


def forward_kernel(x0_ref, x1_ref, pm_ref, zm_ref, s_ref, out_ref, x_buf, a_ref, xs_ref, sem, out_sem):
    for zb in range(8):
        for c in fetch(x0_ref, x1_ref, x_buf, sem, zb):
            c.start()
    w_hi, w_lo = split(phi_table(pm_ref))
    w2 = cat([w_hi, w_lo], 0)
    shape = (128, 128)
    turn = (iota(shape, 0) % 2 - iota(shape, 1) // 64) * (Z // 4)
    t_hi, t_lo = split(z_table(zm_ref, iota(shape, 1) % 64, turn))
    t3 = cat([t_hi, t_lo, t_hi], 1)

    def arrive(zb):
        for c in fetch(x0_ref, x1_ref, x_buf, sem, zb):
            c.wait()

    def keep(zb):
        rows = pl.ds(pl.multiple_of(zb * 2048, 2048), 2048)
        return pltpu.make_async_copy(xs_ref.at[rows, :], out_ref.at[rows, :], out_sem.at[zb])

    arrive(0)

    def block(zb, carry):
        @pl.when(zb < 7)
        def _():
            arrive(zb + 1)

        base = pl.multiple_of(zb * 1024, 1024)
        base2 = pl.multiple_of(zb * 2048, 2048)
        for i in range(4):
            for n in range(2):
                hi, lo = split(stack_z(x_buf, zb, i * 2 + n))
                xs_ref[pl.ds(base2 + (i * 512 + n * 128), 128), :] = hi
                xs_ref[pl.ds(base2 + (i * 512 + 256 + n * 128), 128), :] = lo
            hi = xs_ref[pl.ds(base2 + i * 512, 256), :]
            lo = xs_ref[pl.ds(base2 + (i * 512 + 256), 256), :]
            o = nt(w2, hi)
            o = o[:128] + (o[128:] + nt(w_hi, lo))
            for n in range(2):
                a_ref[pl.ds(base + (i * 2 + n), 128, stride=8), :] = o[:, n * 128 : (n + 1) * 128]
        keep(zb).start()
        return carry

    lax.fori_loop(0, 8, block, 0)

    def pair(j, carry):
        base = pl.multiple_of(((j // 4) * 16 + j % 4 * 2) * 8, 16)

        def rows(n):
            return cat([
                a_ref[pl.ds(base + (n * 8 + part * 64 + zb * 1024), 8), :] for part in range(2) for zb in range(8)
            ], 0)

        hi, lo = split(cat([rows(0), rows(1)], 1))
        o = nn(t3, cat([hi, hi, lo], 0))
        spots = places(j)
        for n in range(2):
            for g in range(16):
                s_ref[spots[n][g], :] = o[g * 8 : g * 8 + 8, n * 128 : (n + 1) * 128]
        return carry

    lax.fori_loop(0, 32, pair, 0, unroll=8)
    for zb in range(8):
        keep(zb).wait()


HBM = pl.BlockSpec(memory_space=pltpu.HBM)
VMEM = pl.BlockSpec(memory_space=pltpu.VMEM)


def forward(field, field_tangent, pm, zm):
    packed = jax.ShapeDtypeStruct((16384, FL), BF16)
    return pl.pallas_call(
        forward_kernel,
        out_shape=(jax.ShapeDtypeStruct((8192, 128), F32), packed),
        in_specs=[HBM, HBM, VMEM, VMEM],
        out_specs=(VMEM, HBM),
        scratch_shapes=[
            pltpu.VMEM((32, 64, 8, 128), F32), pltpu.VMEM((8192, 128), F32), pltpu.VMEM((16384, FL), BF16),
            pltpu.SemaphoreType.DMA((32,)), pltpu.SemaphoreType.DMA((8,)),
        ],
        compiler_params=pltpu.CompilerParams(vmem_limit_bytes=VMEM_FORWARD),
        name="forward_kernel",
    )(field, field_tangent, pm, zm)


def mix(x_ref, w_ref, out_ref):
    def pair(ref):
        re = cat([ref[pl.ds(n * 16, 8), :] for n in range(4)], 0)
        im = cat([ref[pl.ds(n * 16 + 8, 8), :] for n in range(4)], 0)
        return re * SCALE, im * SCALE

    xr, xi = pair(x_ref)
    lane = iota((32, 128), 1) % 64
    gr = jnp.zeros((32, 128), F32)
    gi = jnp.zeros((32, 128), F32)
    for d in range(16):
        if d == 0:
            ar, ai = xr, xi
        else:
            near = lane < 64 - 4 * d
            ar = jnp.where(near, pltpu.roll(xr, 128 - 4 * d, 1), pltpu.roll(xr, 64 - 4 * d, 1))
            ai = jnp.where(near, pltpu.roll(xi, 128 - 4 * d, 1), pltpu.roll(xi, 64 - 4 * d, 1))
        wr = w_ref[pl.ds(d * 64, 32), :]
        wi = w_ref[pl.ds(d * 64 + 32, 32), :]
        gr = gr + (ar * wr - ai * wi)
        gi = gi + (ai * wr + ar * wi)
    for n in range(4):
        out_ref[pl.ds(n * 16, 8), :] = gr[n * 8 : n * 8 + 8]
        out_ref[pl.ds(n * 16 + 8, 8), :] = gi[n * 8 : n * 8 + 8]


def exchange_kernel(
    s_ref, w_ref, g_ref,
    peer, acc, relay, fin, second, rec2, third, rec3, own, gath3,
    pair_s, pair_r, st1_s, st1_r, st2_s, st2_r, st3_s, st3_r,
    ag3_s, ag3_r, ag2_s, ag2_r, ag1_s, ag1_r, hand_s, hand_r,
):
    gz = lax.axis_index("gz")
    x = lax.axis_index("phi")
    core = gz % 2
    z = (gz // 2) % 4
    y = gz // 8

    def device(xx, yy, zz, cc):
        return ((yy * 4 + zz) * 2 + cc, xx)

    pa = x + core * (y - x)
    pb = z
    pd = y + core * (x - y)

    def along_a(t):
        n = (pa + t) % 4
        return device(n + core * (x - n), y + core * (n - y), z, core)

    def along_b(t):
        return device(x, y, (z + t) % 4, core)

    def along_d(t):
        n = (pd + t) % 4
        return device(x + core * (n - x), n + core * (y - n), z, core)

    partner = device(x, y, z, 1 - core)

    sent = []

    def send(src, dst, ss, rs, dev):
        c = pltpu.make_async_remote_copy(
            src_ref=src, dst_ref=dst, send_sem=ss, recv_sem=rs, device_id=dev, device_id_type=MESH
        )
        c.start()
        sent.append(c)
        return c

    right, left = along_a(1), along_a(3)
    barrier = pltpu.get_barrier_semaphore()
    peers = [partner, right, left]
    peers += [along_b(t) for t in (1, 2, 3)] + [along_d(t) for t in (1, 2, 3)]
    for dev in peers:
        pl.semaphore_signal(barrier, inc=1, device_id=dev, device_id_type=MESH)
    pl.semaphore_wait(barrier, 9)

    def mine(t):
        return (pa + t) % 4

    qa = y + core * (x - y)
    order = (2, 1, 3, 0)
    pairs = []
    for n, t in enumerate(order):
        pairs.append(send(s_ref.at[1 - core, (qa + t) % 4], peer.at[n], pair_s.at[n], pair_r.at[n], partner))

    def land(n):
        pairs[n].wait_recv()
        acc[n] = s_ref[core, mine(order[n])] + peer[n]

    def piece(slab, s, h, size=4):
        return acc.at[slab, pl.ds(h * 4, size), (pb + s) % 4]

    turns = (2, 1, 3, 0)
    land(0)
    relays = {}
    for s in turns:
        n = s * 6
        relays[0, s] = send(piece(0, s, 0), relay.at[0, s], st1_s.at[n], st1_r.at[n], right)
        relays[1, s] = send(piece(0, s, 1), relay.at[1, s], st1_s.at[n + 1], st1_r.at[n + 1], left)
    land(1)
    land(2)
    first = {}
    for s in turns:
        n = s * 6
        first[s] = [
            send(piece(1, s, 1), fin.at[0, s, pl.ds(4, 4)], st1_s.at[n + 2], st1_r.at[n + 2], right),
            send(piece(2, s, 0), fin.at[1, s, pl.ds(0, 4)], st1_s.at[n + 3], st1_r.at[n + 3], left),
        ]
        for side, dev in enumerate((right, left)):
            relays[side, s].wait_recv()
            ref = piece(1 + side, s, side)
            ref[...] = ref[...] + relay[side, s]
            dst = fin.at[side, s, pl.ds(side * 4, 4)]
            first[s].append(send(ref, dst, st1_s.at[n + 4 + side], st1_r.at[n + 4 + side], dev))
    land(3)

    sends2 = []
    for s in turns:
        for c in first[s]:
            c.wait_recv()
        second[s] = piece(3, s, 0, 8)[...] + (fin[0, s] + fin[1, s])
        if s:
            sends2.append(send(second.at[s], rec2.at[s - 1], st2_s.at[s - 1], st2_r.at[s - 1], along_b(s)))
    for c in sends2:
        c.wait_recv()
    third[...] = (second[0] + rec2[0] + (rec2[1] + rec2[2])).reshape(4, 64, 128)

    sends3 = []
    for t in turns[:3]:
        sends3.append(send(third.at[(pd + t) % 4], rec3.at[t - 1], st3_s.at[t - 1], st3_r.at[t - 1], along_d(t)))
    for c in sends3:
        c.wait_recv()
    own[...] = third[pd] + rec3[0] + (rec3[1] + rec3[2])
    mine3 = gath3.at[pd]
    mix(own, w_ref, mine3)

    gat3 = [send(mine3, mine3, ag3_s.at[t - 1], ag3_r.at[t - 1], along_d(t)) for t in turns[:3]]
    for c in gat3:
        c.wait_recv()

    def spot(t, s, h, size=4):
        return g_ref.at[core, mine(t), pl.ds(h * 4, size), (pb + s) % 4]

    mine2 = spot(0, 0, 0, 8)
    mine2[...] = gath3[...].reshape(8, 32, 128)

    gat2 = {t: send(mine2, mine2, ag2_s.at[t - 1], ag2_r.at[t - 1], along_b(t)) for t in (1, 3, 2)}
    gat1 = {}
    hands = []

    def pass_on(u, key, t, h, dev):
        n = u * 6 + ("ra", "lb", "rb", "la", "fr", "fl").index(key)
        gat1[u, key] = send(spot(t, u, h), spot(t, u, h), ag1_s.at[n], ag1_r.at[n], dev)

    def hand(u, n, t, h, size=4):
        ref = spot(t, u, h, size)
        hands.append(send(ref, ref, hand_s.at[u * 7 + n], hand_r.at[u * 7 + n], partner))

    def emit(u):
        pass_on(u, "ra", 0, 0, right)
        pass_on(u, "lb", 0, 1, left)
        pass_on(u, "rb", 0, 1, right)
        pass_on(u, "la", 0, 0, left)
        hand(u, 0, 0, 0, 8)

    def turn_round(u):
        gat1[u, "ra"].wait_recv()
        pass_on(u, "fr", 3, 0, right)
        gat1[u, "lb"].wait_recv()
        pass_on(u, "fl", 1, 1, left)
        hand(u, 1, 3, 0)
        hand(u, 2, 1, 1)

    emit(0)
    gat2[1].wait_recv()
    emit(3)
    turn_round(0)
    gat2[3].wait_recv()
    emit(1)
    turn_round(3)
    gat2[2].wait_recv()
    emit(2)
    turn_round(1)
    turn_round(2)
    for u in (0, 3, 1, 2):
        gat1[u, "rb"].wait_recv()
        hand(u, 3, 3, 1)
        gat1[u, "la"].wait_recv()
        hand(u, 4, 1, 0)
        gat1[u, "fr"].wait_recv()
        hand(u, 5, 2, 0)
        gat1[u, "fl"].wait_recv()
        hand(u, 6, 2, 1)
    for c in hands:
        c.wait_recv()
    for c in sent:
        c.wait_send()


def exchange(s, w):
    dma = pltpu.SemaphoreType.DMA
    buf = lambda *dims: pltpu.VMEM((*dims, 128), F32)
    return pl.pallas_call(
        exchange_kernel,
        out_shape=jax.ShapeDtypeStruct((2, 4, 8, 4, 32, 128), F32),
        in_specs=[VMEM, VMEM],
        out_specs=VMEM,
        scratch_shapes=[
            buf(4, 8, 4, 32), buf(4, 8, 4, 32), buf(2, 4, 4, 32), buf(2, 4, 8, 32), buf(4, 8, 32), buf(3, 8, 32),
            buf(4, 64), buf(3, 64), buf(64), buf(4, 64),
            dma((4,)), dma((4,)), dma((24,)), dma((24,)), dma((3,)), dma((3,)), dma((3,)), dma((3,)),
            dma((3,)), dma((3,)), dma((3,)), dma((3,)), dma((24,)), dma((24,)), dma((28,)), dma((28,)),
        ],
        compiler_params=pltpu.CompilerParams(collective_id=0, has_side_effects=True, vmem_limit_bytes=VMEM_EXCHANGE),
        name="exchange_kernel",
    )(s.reshape(2, 4, 8, 4, 32, 128), w).reshape(8192, 128)


def inverse_kernel(
    xs_ref, g_ref, pm_ref, zm_ref, lw_ref, bias_ref, o_ref, t_ref, u_ref, acc_ref, out_buf, out_sem
):
    shape = (128, 128)
    row, col = iota(shape, 0), iota(shape, 1)
    turn = (row % 2 - col % 2) * (Z // 4)
    t_hi, t_lo = split(z_table(zm_ref, col // 2, turn).T)
    t3 = cat([t_hi, t_lo, t_hi], 1)

    def pair(j, carry):
        spots = places(j)
        g2 = cat([cat([g_ref[spots[n][g], :] for g in range(16)], 0) for n in range(2)], 1)
        hi, lo = split(g2)
        o = nn(t3, cat([hi, hi, lo], 0))
        base = (j // 4) * 1024 + j % 4 * 2
        for n in range(2):
            for g in range(16):
                u_ref[pl.ds(base + (n + g * 64), 8, stride=8), :] = o[g * 8 : g * 8 + 8, n * 128 : (n + 1) * 128]
        return carry

    lax.fori_loop(0, 32, pair, 0, unroll=8)
    v_hi, v_lo = split(phi_table(pm_ref))
    pick = (iota((128, 16), 0) // 4 % 16 == iota((128, 16), 1)).astype(F32)
    full = lax.Precision.HIGHEST
    rows = lax.dot_general(pick, lw_ref[...], (((1,), (1,)), ((), ())), precision=full, preferred_element_type=F32)
    grid = lax.dot_general(rows, pick, (((1,), (1,)), ((), ())), precision=full, preferred_element_type=F32)
    same = (row // 64 == col // 64) & (row % 4 == col % 4)
    l_hi, l_lo = split(jnp.where(same, grid, 0.0))
    bias = jnp.sum(jnp.where(iota((64, 16), 0) // 4 == iota((64, 16), 1), bias_ref[...], 0.0), axis=1, keepdims=True)
    c0 = math.sqrt(2.0 / math.pi)

    def copies(zb, slot):
        out = []
        for n, dst in enumerate((o_ref, t_ref)):
            for h in range(2):
                out.append(pltpu.make_async_copy(
                    out_buf.at[slot * 4 + n * 2 + h], dst.at[:, pl.ds(pl.multiple_of(zb * 8, 8), 8), pl.ds(h * 128, 128)],
                    out_sem.at[slot * 4 + n * 2 + h],
                ))
        return out

    def gather_z(z, slot):
        z16 = z * 16
        u = cat([u_ref[pl.ds(pl.multiple_of(n * 1024 + z16, 16), 16), :] for n in range(8)], 0)
        u_hi, u_lo = split(u.T)
        zrow = (z // 2) * 512 + (z % 2) * 128
        hi = xs_ref[pl.ds(pl.multiple_of(zrow, 128), 128), :]
        lo = xs_ref[pl.ds(pl.multiple_of(zrow + 256, 128), 128), :]
        acc_ref[slot] = nn(cat([u_hi, u_lo, u_hi, l_hi, l_lo, l_hi], 1), cat([v_hi, v_hi, v_lo, hi, hi, lo], 0))

    gather_z(0, 0)

    def block(zb, carry):
        slot = zb % 2

        @pl.when(zb >= 2)
        def _():
            for c in copies(zb, slot):
                c.wait()

        flat = out_buf.reshape(8 * 512, 128)
        for i in range(8):
            gather_z(jnp.minimum(zb * 8 + i + 1, 63), (i + 1) % 2)
            pre = acc_ref[i % 2, 0:64, :] + bias
            tan = acc_ref[i % 2, 64:128, :]
            sq = pre * pre
            t = jnp.tanh(pre * (c0 + (c0 * 0.044715) * sq))
            half = 0.5 + 0.5 * t
            slope = half + (0.5 * pre) * ((1.0 - t * t) * (c0 + (3.0 * 0.044715 * c0) * sq))
            for n, val in enumerate((pre * half, slope * tan)):
                for h in range(2):
                    flat[pl.ds(slot * 2048 + n * 1024 + h * 512 + i, 64, stride=8), :] = val[:, h * 128 : (h + 1) * 128]
        for c in copies(zb, slot):
            c.start()
        return carry

    lax.fori_loop(0, 8, block, 0)
    for zb in (6, 7):
        for c in copies(zb, zb % 2):
            c.wait()


def inverse(xs, g, pm, zm, lw, bias):
    out = jax.ShapeDtypeStruct((64, ZL, FL), F32)
    return pl.pallas_call(
        inverse_kernel,
        out_shape=(out, out),
        in_specs=[VMEM, VMEM, VMEM, VMEM, VMEM, VMEM],
        out_specs=(HBM, HBM),
        scratch_shapes=[
            pltpu.VMEM((8192, 128), F32), pltpu.VMEM((2, 128, FL), F32), pltpu.VMEM((8, 64, 8, 128), F32),
            pltpu.SemaphoreType.DMA((8,)),
        ],
        compiler_params=pltpu.CompilerParams(vmem_limit_bytes=VMEM_INVERSE),
        name="inverse_kernel",
    )(xs, g, pm, zm, lw, bias)


def body(field, field_tangent, spectral_weight, local_weight, bias_term, z_modes, phi_modes):
    x0 = field.reshape(64, ZL, FL)
    x1 = field_tangent.reshape(64, ZL, FL)
    zm = z_modes.reshape(1, 64)
    pm = phi_modes.reshape(1, 64)
    w = spectral_weight.reshape(2, 16, 16, 2, 2, 8)
    c, o, d, lane = (lax.broadcasted_iota(I32, (16, 16, 16, 128), n) for n in range(4))
    lane_o = lane // 4 % 16
    pick = ((o == lane_o) & (c == (lane_o + d) % 16)).astype(F32)
    wd = jnp.einsum("icokhq,codl->dihkql", w, pick, precision=lax.Precision.HIGHEST).reshape(1024, 128)
    s, xs = forward(x0, x1, pm, zm)
    g = exchange(s, wd)
    out, tan = inverse(xs, g, pm, zm, local_weight, bias_term.reshape(1, 16))
    return out.reshape(16, 4, ZL, FL), tan.reshape(16, 4, ZL, FL)


def solution(mesh):
    return jax.shard_map(
        body,
        mesh=mesh,
        in_specs=(
            P(None, None, "gz", "phi"),
            P(None, None, "gz", "phi"),
            P(None, None, None, "gz", "phi"),
            P(),
            P(),
            P(),
            P(),
        ),
        out_specs=(P(None, None, "gz", "phi"), P(None, None, "gz", "phi")),
        check_vma=False,
    )
```

profile of v0, /device:TPU:1, one launch (start us, length us, event | category | flops | bytes accessed | tf_op | source)
XLA Modules:
  0.0 75.4 jit_solution(6713700117576691121)
XLA Ops:
  0.7 1.2 %copy.11 = f32[2,16,16,2,16]{2,4,3,1,0:T(8,128)S(1)} copy(f32[2,16,16,2,16]{4,3,2,1,0:T(2,128)} %param.9) | data formatting | bytes 131072 | tf_op args[2]
  1.9 0.0 copy-start.2
  1.9 0.0 copy-start.3
  1.9 0.9 %fusion.15 = f32[16,2,2,2,8,128]{5,4,2,3,1,0:T(8,128)S(1)} fusion(s32[128]{0:T(128)S(1)} %get-tuple-element.10, s32[128]{0:T(128)S(1)} %get-tuple-element.11, pred[128]{0:T(512)(128)(4,1)S(1)} %compare_and_fusion, f32[2,16,16,2,16]{2,4,3,1,0:T(8,128)S(1)} %copy.11), kind=kOutput, calls=%fused_computation.21 | convolution fusion | flops 416808960 | bytes 590976 | tf_op jit(solution)/shard_map/icokhq,codl->dihkql/dot_general | solution.py:508
  2.9 0.0 copy-done.2
  2.9 0.0 copy-done.3
  2.9 9.8 %forward_kernel.1 = (f32[8192,128]{1,0:T(8,128)S(1)}, bf16[16384,256]{1,0:T(8,128)(2,1)}) custom-call(f32[64,64,256]{2,1,0:T(8,128)} %bitcast.37, f32[64,64,256]{2,1,0:T(8,128)} %bitcast.38, s32[1,64]{1,0:T(1,128)S(1)} %bitcast.32, s32[1,64]{1,0:T(1,128)S(1)} %bitcast.34), custom_call_target="tpu_custom_call" | custom-call | tf_op jit(solution)/shard_map/forward_kernel/pallas_call | solution.py:169
  12.8 0.0 copy-start
  12.8 0.0 copy-start.1
  12.8 0.0 copy-start.4
  12.8 51.6 %exchange_kernel.1 = f32[2,4,8,4,32,128]{5,4,3,2,1,0:T(8,128)S(1)} custom-call(f32[2,4,8,4,32,128]{5,4,3,2,1,0:T(8,128)S(1)} %bitcast.30, f32[1024,128]{1,0:T(8,128)S(1)} %bitcast.31), custom_call_target="tpu_custom_call" | custom-call | tf_op jit(solution)/shard_map/exchange_kernel/pallas_call | solution.py:385
  64.4 0.0 copy-done
  64.4 0.0 copy-done.1
  64.5 0.0 copy-done.4
  64.5 11.0 %inverse_kernel.1 = (f32[64,64,256]{2,1,0:T(8,128)}, f32[64,64,256]{2,1,0:T(8,128)}) custom-call(bf16[16384,256]{1,0:T(8,128)(2,1)S(1)} %copy-done, f32[8192,128]{1,0:T(8,128)S(1)} %bitcast.29, s32[1,64]{1,0:T(1,128)S(1)} %bitcast.33, s32[1,64]{1,0:T(1,128)S(1)} %bitcast.35, f32[16,16]{1,0:T(8,128)S(1)} %copy-done.1, f32[1,16]{1,0:T(1,128)S(1)} %bitcast.36), custom_call_target="tpu_custom_call" | custom-call | tf_op jit(solution)/shard_map/inverse_kernel/pallas_call | solution.py:485
  (3 shorter events, 0.1 us)
Async XLA Ops:
  1.9 1.0 %copy-start.2 = (s32[64]{0:T(128)S(1)}, s32[64]{0:T(128)}, u32[]{:S(2)}) copy-start(s32[64]{0:T(128)} %param.13) | copy-start | bytes 772
  1.9 1.0 %copy-start.3 = (s32[64]{0:T(128)S(1)}, s32[64]{0:T(128)}, u32[]{:S(2)}) copy-start(s32[64]{0:T(128)} %param.12) | copy-start | bytes 772
  12.8 51.7 %copy-start = (bf16[16384,256]{1,0:T(8,128)(2,1)S(1)}, bf16[16384,256]{1,0:T(8,128)(2,1)}, u32[]{:S(2)}) copy-start(bf16[16384,256]{1,0:T(8,128)(2,1)} %get-tuple-element.6.xs_ref) | copy-start | bytes 25165828
  12.8 51.7 %copy-start.1 = (f32[16,16]{1,0:T(8,128)S(1)}, f32[16,16]{1,0:T(8,128)}, u32[]{:S(2)}) copy-start(f32[16,16]{1,0:T(8,128)} %lw_ref.1) | copy-start | bytes 3076
  12.8 51.7 %copy-start.4 = (f32[16]{0:T(128)S(1)}, f32[16]{0:T(128)}, u32[]{:S(2)}) copy-start(f32[16]{0:T(128)} %param.11) | copy-start | bytes 196
where the time goes:
time: 75.6 us; the launch traced here: 75.4 us
  Pallas kernels  72.4 us (96%)
  local copies, waits for them, and re-layouts  1.31 us (2%)
  matrix products  0.92 us (1%)
    pallas_call x1, Pallas kernels, exchange(): pl.pallas_call(exchange_kernel, out_shape=jax.ShapeDtypeStruct((2, 4, 8,...  51.6 us
    pallas_call x1, Pallas kernels, inverse(): pl.pallas_call(inverse_kernel, out_shape=(out, out), in_specs=[VMEM, VMEM...  11 us
    pallas_call x1, Pallas kernels, forward(): pl.pallas_call(forward_kernel, out_shape=(jax.ShapeDtypeStruct((8192, 128...  9.84 us

commit v1 on v0

--- a/solution.py
+++ b/solution.py
@@ -12,9 +12,8 @@
 Z, PHI, KZ, KP = 2048, 1024, 64, 64
 F32, BF16, I32 = jnp.float32, jnp.bfloat16, jnp.int32
 MESH = pl.DeviceIdType.MESH
-VMEM_FORWARD = 48 << 20
-VMEM_EXCHANGE = 24 << 20
-VMEM_INVERSE = 24 << 20
+VMEM_EXCHANGE = 46 << 20
+VMEM_INVERSE = 44 << 20
 SCALE = (1.0 / math.sqrt(Z * PHI)) * (2.0 / math.sqrt(KZ * KP))
 
 
@@ -95,12 +94,13 @@
     return jnp.concatenate(parts, axis=axis)
 
 
-def forward_kernel(x0_ref, x1_ref, pm_ref, zm_ref, s_ref, out_ref, x_buf, a_ref, xs_ref, sem, out_sem):
+def transform(x0_ref, x1_ref, pm_ref, zm_ref, s_ref, x_buf, a_ref, xs_ref, v_ref, sem):
     for zb in range(8):
         for c in fetch(x0_ref, x1_ref, x_buf, sem, zb):
             c.start()
     w_hi, w_lo = split(phi_table(pm_ref))
     w2 = cat([w_hi, w_lo], 0)
+    v_ref[...] = w2
     shape = (128, 128)
     turn = (iota(shape, 0) % 2 - iota(shape, 1) // 64) * (Z // 4)
     t_hi, t_lo = split(z_table(zm_ref, iota(shape, 1) % 64, turn))
@@ -109,10 +109,6 @@
     def arrive(zb):
         for c in fetch(x0_ref, x1_ref, x_buf, sem, zb):
             c.wait()
-
-    def keep(zb):
-        rows = pl.ds(pl.multiple_of(zb * 2048, 2048), 2048)
-        return pltpu.make_async_copy(xs_ref.at[rows, :], out_ref.at[rows, :], out_sem.at[zb])
 
     arrive(0)
 
@@ -134,7 +130,6 @@
             o = o[:128] + (o[128:] + nt(w_hi, lo))
             for n in range(2):
                 a_ref[pl.ds(base + (i * 2 + n), 128, stride=8), :] = o[:, n * 128 : (n + 1) * 128]
-        keep(zb).start()
         return carry
 
     lax.fori_loop(0, 8, block, 0)
@@ -156,28 +151,31 @@
         return carry
 
     lax.fori_loop(0, 32, pair, 0, unroll=8)
-    for zb in range(8):
-        keep(zb).wait()
+
+
+def inverse_z(modes_ref, t_ref):
+    row, col = iota((128, 128), 0), iota((128, 128), 1)
+    turn = (row % 2 - col % 2) * (Z // 4)
+    hi, lo = split(z_table(modes_ref, col // 2, turn).T)
+    t_ref[:, 0:128] = hi
+    t_ref[:, 128:256] = lo
+
+
+def local_mixing(lw_ref, bias_ref):
+    pick = (iota((128, 16), 0) // 4 % 16 == iota((128, 16), 1)).astype(F32)
+    full = lax.Precision.HIGHEST
+    rows = lax.dot_general(pick, lw_ref[...], (((1,), (1,)), ((), ())), precision=full, preferred_element_type=F32)
+    grid = lax.dot_general(rows, pick, (((1,), (1,)), ((), ())), precision=full, preferred_element_type=F32)
+    row, col = iota((128, 128), 0), iota((128, 128), 1)
+    same = (row // 64 == col // 64) & (row % 4 == col % 4)
+    l_hi, l_lo = split(jnp.where(same, grid, 0.0))
+    here = (iota((128, 16), 0) // 4 == iota((128, 16), 1))
+    bias = jnp.sum(jnp.where(here, bias_ref[...], 0.0), axis=1, keepdims=True)
+    return cat([l_hi, l_lo, l_hi], 1), bias
 
 
 HBM = pl.BlockSpec(memory_space=pltpu.HBM)
 VMEM = pl.BlockSpec(memory_space=pltpu.VMEM)
-
-
-def forward(field, field_tangent, pm, zm):
-    packed = jax.ShapeDtypeStruct((16384, FL), BF16)
-    return pl.pallas_call(
-        forward_kernel,
-        out_shape=(jax.ShapeDtypeStruct((8192, 128), F32), packed),
-        in_specs=[HBM, HBM, VMEM, VMEM],
-        out_specs=(VMEM, HBM),
-        scratch_shapes=[
-            pltpu.VMEM((32, 64, 8, 128), F32), pltpu.VMEM((8192, 128), F32), pltpu.VMEM((16384, FL), BF16),
-            pltpu.SemaphoreType.DMA((32,)), pltpu.SemaphoreType.DMA((8,)),
-        ],
-        compiler_params=pltpu.CompilerParams(vmem_limit_bytes=VMEM_FORWARD),
-        name="forward_kernel",
-    )(field, field_tangent, pm, zm)
 
 
 def mix(x_ref, w_ref, out_ref):
@@ -207,8 +205,8 @@
 
 
 def exchange_kernel(
-    s_ref, w_ref, g_ref,
-    peer, acc, relay, fin, second, rec2, third, rec3, own, gath3,
+    x0_ref, x1_ref, pm_ref, zm_ref, w_ref, lw_ref, bias_ref, g_ref, loc_ref, v_ref, t_ref,
+    x_buf, a_ref, xs_ref, spec_ref, loc_buf, x_sem, loc_sem, peer, acc, relay, fin, second, relay2, rec2, third, rec3, own, gath3,
     pair_s, pair_r, st1_s, st1_r, st2_s, st2_r, st3_s, st3_r,
     ag3_s, ag3_r, ag2_s, ag2_r, ag1_s, ag1_r, hand_s, hand_r,
 ):
@@ -251,10 +249,12 @@
     right, left = along_a(1), along_a(3)
     barrier = pltpu.get_barrier_semaphore()
     peers = [partner, right, left]
-    peers += [along_b(t) for t in (1, 2, 3)] + [along_d(t) for t in (1, 2, 3)]
+    peers += [along_b(1), along_b(3)] + [along_d(t) for t in (1, 2, 3)]
     for dev in peers:
         pl.semaphore_signal(barrier, inc=1, device_id=dev, device_id_type=MESH)
-    pl.semaphore_wait(barrier, 9)
+    transform(x0_ref, x1_ref, pm_ref, zm_ref, spec_ref, x_buf, a_ref, xs_ref, v_ref, x_sem)
+    s_ref = spec_ref.reshape(2, 4, 8, 4, 32, 128)
+    pl.semaphore_wait(barrier, 8)
 
     def mine(t):
         return (pa + t) % 4
@@ -264,6 +264,31 @@
     pairs = []
     for n, t in enumerate(order):
         pairs.append(send(s_ref.at[1 - core, (qa + t) % 4], peer.at[n], pair_s.at[n], pair_r.at[n], partner))
+
+    l3, bias = local_mixing(lw_ref, bias_ref)
+    stores = []
+
+    def mix_local(zb):
+        slot = zb % 2
+        if zb >= 2:
+            stores[zb - 2].wait()
+
+        def four(i, carry):
+            for n in range(4):
+                row = (zb * 4 + n // 2) * 512 + n % 2 * 128
+                hi = xs_ref[pl.ds(pl.multiple_of(i * 1024 + row, 128), 128), :]
+                lo = xs_ref[pl.ds(pl.multiple_of(i * 1024 + row + 256, 128), 128), :]
+                o = nn(l3, cat([hi, hi, lo], 0)) + bias
+                loc_buf[slot, pl.ds(pl.multiple_of(i * 512 + n * 128, 128), 128), :] = o
+            return carry
+
+        lax.fori_loop(0, 2, four, 0)
+        c = pltpu.make_async_copy(loc_buf.at[slot], loc_ref.at[pl.ds(zb * 1024, 1024), :], loc_sem.at[zb])
+        c.start()
+        stores.append(c)
+
+    mix_local(0)
+    mix_local(1)
 
     def land(n):
         pairs[n].wait_recv()
@@ -279,6 +304,7 @@
         n = s * 6
         relays[0, s] = send(piece(0, s, 0), relay.at[0, s], st1_s.at[n], st1_r.at[n], right)
         relays[1, s] = send(piece(0, s, 1), relay.at[1, s], st1_s.at[n + 1], st1_r.at[n + 1], left)
+    mix_local(2)
     land(1)
     land(2)
     first = {}
@@ -288,6 +314,7 @@
             send(piece(1, s, 1), fin.at[0, s, pl.ds(4, 4)], st1_s.at[n + 2], st1_r.at[n + 2], right),
             send(piece(2, s, 0), fin.at[1, s, pl.ds(0, 4)], st1_s.at[n + 3], st1_r.at[n + 3], left),
         ]
+        mix_local(3 + turns.index(s))
         for side, dev in enumerate((right, left)):
             relays[side, s].wait_recv()
             ref = piece(1 + side, s, side)
@@ -301,11 +328,21 @@
         for c in first[s]:
             c.wait_recv()
         second[s] = piece(3, s, 0, 8)[...] + (fin[0, s] + fin[1, s])
-        if s:
-            sends2.append(send(second.at[s], rec2.at[s - 1], st2_s.at[s - 1], st2_r.at[s - 1], along_b(s)))
+        if s == 2:
+            far = [
+                send(second.at[2, pl.ds(h * 4, 4)], relay2.at[h], st2_s.at[h], st2_r.at[h], along_b(1 + 2 * h))
+                for h in range(2)
+            ]
+        elif s:
+            h = s // 2
+            far[h].wait_recv()
+            part = second.at[s, pl.ds(h * 4, 4)]
+            part[...] = part[...] + relay2[h]
+            sends2.append(send(second.at[s], rec2.at[h], st2_s.at[2 + h], st2_r.at[2 + h], along_b(s)))
+    mix_local(7)
     for c in sends2:
         c.wait_recv()
-    third[...] = (second[0] + rec2[0] + (rec2[1] + rec2[2])).reshape(4, 64, 128)
+    third[...] = (second[0] + (rec2[0] + rec2[1])).reshape(4, 64, 128)
 
     sends3 = []
     for t in turns[:3]:
@@ -317,6 +354,7 @@
     mix(own, w_ref, mine3)
 
     gat3 = [send(mine3, mine3, ag3_s.at[t - 1], ag3_r.at[t - 1], along_d(t)) for t in turns[:3]]
+    inverse_z(zm_ref, t_ref)
     for c in gat3:
         c.wait_recv()
 
@@ -326,85 +364,112 @@
     mine2 = spot(0, 0, 0, 8)
     mine2[...] = gath3[...].reshape(8, 32, 128)
 
-    gat2 = {t: send(mine2, mine2, ag2_s.at[t - 1], ag2_r.at[t - 1], along_b(t)) for t in (1, 3, 2)}
-    gat1 = {}
-    hands = []
-
-    def pass_on(u, key, t, h, dev):
+    gat2, gat1, hands = {}, {}, []
+
+    def pass_b(key, u, h, t):
+        n = ("ra", "lb", "rb", "la", "fr", "fl").index(key)
+        gat2[key] = send(spot(0, u, h), spot(0, u, h), ag2_s.at[n], ag2_r.at[n], along_b(t))
+
+    def pass_a(key, u, t, h, dev):
         n = u * 6 + ("ra", "lb", "rb", "la", "fr", "fl").index(key)
         gat1[u, key] = send(spot(t, u, h), spot(t, u, h), ag1_s.at[n], ag1_r.at[n], dev)
 
-    def hand(u, n, t, h, size=4):
-        ref = spot(t, u, h, size)
-        hands.append(send(ref, ref, hand_s.at[u * 7 + n], hand_r.at[u * 7 + n], partner))
-
-    def emit(u):
-        pass_on(u, "ra", 0, 0, right)
-        pass_on(u, "lb", 0, 1, left)
-        pass_on(u, "rb", 0, 1, right)
-        pass_on(u, "la", 0, 0, left)
-        hand(u, 0, 0, 0, 8)
+    def hand(u, n, t, h):
+        ref = spot(t, u, h)
+        hands.append(send(ref, ref, hand_s.at[u * 8 + n], hand_r.at[u * 8 + n], partner))
+
+    def emit(u, h):
+        if h == 0:
+            pass_a("ra", u, 0, 0, right)
+            pass_a("la", u, 0, 0, left)
+        else:
+            pass_a("lb", u, 0, 1, left)
+            pass_a("rb", u, 0, 1, right)
+        hand(u, h, 0, h)
 
     def turn_round(u):
         gat1[u, "ra"].wait_recv()
-        pass_on(u, "fr", 3, 0, right)
+        pass_a("fr", u, 3, 0, right)
         gat1[u, "lb"].wait_recv()
-        pass_on(u, "fl", 1, 1, left)
-        hand(u, 1, 3, 0)
-        hand(u, 2, 1, 1)
-
-    emit(0)
-    gat2[1].wait_recv()
-    emit(3)
+        pass_a("fl", u, 1, 1, left)
+        hand(u, 2, 3, 0)
+        hand(u, 3, 1, 1)
+
+    pass_b("ra", 0, 0, 1)
+    pass_b("lb", 0, 1, 3)
+    pass_b("rb", 0, 1, 1)
+    pass_b("la", 0, 0, 3)
+    emit(0, 0)
+    emit(0, 1)
+    gat2["ra"].wait_recv()
+    pass_b("fr", 3, 0, 1)
+    gat2["lb"].wait_recv()
+    pass_b("fl", 1, 1, 3)
+    emit(3, 0)
+    emit(1, 1)
     turn_round(0)
-    gat2[3].wait_recv()
-    emit(1)
-    turn_round(3)
-    gat2[2].wait_recv()
-    emit(2)
-    turn_round(1)
-    turn_round(2)
+    gat2["rb"].wait_recv()
+    emit(3, 1)
+    gat2["la"].wait_recv()
+    emit(1, 0)
+    gat2["fr"].wait_recv()
+    emit(2, 0)
+    gat2["fl"].wait_recv()
+    emit(2, 1)
+    for u in (3, 1, 2):
+        turn_round(u)
     for u in (0, 3, 1, 2):
         gat1[u, "rb"].wait_recv()
-        hand(u, 3, 3, 1)
+        hand(u, 4, 3, 1)
         gat1[u, "la"].wait_recv()
-        hand(u, 4, 1, 0)
+        hand(u, 5, 1, 0)
         gat1[u, "fr"].wait_recv()
-        hand(u, 5, 2, 0)
+        hand(u, 6, 2, 0)
         gat1[u, "fl"].wait_recv()
-        hand(u, 6, 2, 1)
+        hand(u, 7, 2, 1)
     for c in hands:
         c.wait_recv()
     for c in sent:
         c.wait_send()
-
-
-def exchange(s, w):
+    for c in stores[6:]:
+        c.wait()
+
+
+def exchange(field, field_tangent, pm, zm, wt, lw, bias):
     dma = pltpu.SemaphoreType.DMA
     buf = lambda *dims: pltpu.VMEM((*dims, 128), F32)
+    table = jax.ShapeDtypeStruct((256, 256), BF16)
     return pl.pallas_call(
         exchange_kernel,
-        out_shape=jax.ShapeDtypeStruct((2, 4, 8, 4, 32, 128), F32),
-        in_specs=[VMEM, VMEM],
-        out_specs=VMEM,
+        out_shape=(
+            jax.ShapeDtypeStruct((2, 4, 8, 4, 32, 128), F32), jax.ShapeDtypeStruct((8192, FL), F32),
+            table, jax.ShapeDtypeStruct((128, 256), BF16),
+        ),
+        in_specs=[HBM, HBM, VMEM, VMEM, VMEM, VMEM, VMEM],
+        out_specs=(VMEM, HBM, VMEM, VMEM),
         scratch_shapes=[
-            buf(4, 8, 4, 32), buf(4, 8, 4, 32), buf(2, 4, 4, 32), buf(2, 4, 8, 32), buf(4, 8, 32), buf(3, 8, 32),
+            buf(32, 64, 8), buf(8192), pltpu.VMEM((16384, FL), BF16), buf(8192),
+            pltpu.VMEM((2, 1024, FL), F32), dma((32,)), dma((8,)),
+            buf(4, 8, 4, 32), buf(4, 8, 4, 32), buf(2, 4, 4, 32), buf(2, 4, 8, 32), buf(4, 8, 32), buf(2, 4, 32), buf(2, 8, 32),
             buf(4, 64), buf(3, 64), buf(64), buf(4, 64),
-            dma((4,)), dma((4,)), dma((24,)), dma((24,)), dma((3,)), dma((3,)), dma((3,)), dma((3,)),
-            dma((3,)), dma((3,)), dma((3,)), dma((3,)), dma((24,)), dma((24,)), dma((28,)), dma((28,)),
+            dma((4,)), dma((4,)), dma((24,)), dma((24,)), dma((4,)), dma((4,)), dma((3,)), dma((3,)),
+            dma((3,)), dma((3,)), dma((6,)), dma((6,)), dma((24,)), dma((24,)), dma((32,)), dma((32,)),
         ],
         compiler_params=pltpu.CompilerParams(collective_id=0, has_side_effects=True, vmem_limit_bytes=VMEM_EXCHANGE),
         name="exchange_kernel",
-    )(s.reshape(2, 4, 8, 4, 32, 128), w).reshape(8192, 128)
+    )(field, field_tangent, pm, zm, wt, lw, bias)
 
 
 def inverse_kernel(
-    xs_ref, g_ref, pm_ref, zm_ref, lw_ref, bias_ref, o_ref, t_ref, u_ref, acc_ref, out_buf, out_sem
+    loc_hbm, g_ref, v_ref, tz_ref, o_ref, t_ref, loc_ref, u_ref, acc_ref, out_buf, loc_sem, out_sem
 ):
-    shape = (128, 128)
-    row, col = iota(shape, 0), iota(shape, 1)
-    turn = (row % 2 - col % 2) * (Z // 4)
-    t_hi, t_lo = split(z_table(zm_ref, col // 2, turn).T)
+    def take(zb):
+        rows = pl.ds(pl.multiple_of(zb * 1024, 1024), 1024)
+        return pltpu.make_async_copy(loc_hbm.at[rows, :], loc_ref.at[rows, :], loc_sem.at[zb])
+
+    for zb in range(8):
+        take(zb).start()
+    t_hi, t_lo = tz_ref[:, 0:128], tz_ref[:, 128:256]
     t3 = cat([t_hi, t_lo, t_hi], 1)
 
     def pair(j, carry):
@@ -419,14 +484,8 @@
         return carry
 
     lax.fori_loop(0, 32, pair, 0, unroll=8)
-    v_hi, v_lo = split(phi_table(pm_ref))
-    pick = (iota((128, 16), 0) // 4 % 16 == iota((128, 16), 1)).astype(F32)
-    full = lax.Precision.HIGHEST
-    rows = lax.dot_general(pick, lw_ref[...], (((1,), (1,)), ((), ())), precision=full, preferred_element_type=F32)
-    grid = lax.dot_general(rows, pick, (((1,), (1,)), ((), ())), precision=full, preferred_element_type=F32)
-    same = (row // 64 == col // 64) & (row % 4 == col % 4)
-    l_hi, l_lo = split(jnp.where(same, grid, 0.0))
-    bias = jnp.sum(jnp.where(iota((64, 16), 0) // 4 == iota((64, 16), 1), bias_ref[...], 0.0), axis=1, keepdims=True)
+    v_hi, v_lo = v_ref[0:128, :], v_ref[128:256, :]
+    v3 = cat([v_hi, v_hi, v_lo], 0)
     c0 = math.sqrt(2.0 / math.pi)
 
     def copies(zb, slot):
@@ -443,15 +502,18 @@
         z16 = z * 16
         u = cat([u_ref[pl.ds(pl.multiple_of(n * 1024 + z16, 16), 16), :] for n in range(8)], 0)
         u_hi, u_lo = split(u.T)
-        zrow = (z // 2) * 512 + (z % 2) * 128
-        hi = xs_ref[pl.ds(pl.multiple_of(zrow, 128), 128), :]
-        lo = xs_ref[pl.ds(pl.multiple_of(zrow + 256, 128), 128), :]
-        acc_ref[slot] = nn(cat([u_hi, u_lo, u_hi, l_hi, l_lo, l_hi], 1), cat([v_hi, v_hi, v_lo, hi, hi, lo], 0))
-
+        local = loc_ref[pl.ds(pl.multiple_of(z * 128, 128), 128), :]
+        acc_ref[slot] = nn(cat([u_hi, u_lo, u_hi], 1), v3) + local
+
+    take(0).wait()
     gather_z(0, 0)
 
     def block(zb, carry):
         slot = zb % 2
+
+        @pl.when(zb < 7)
+        def _():
+            take(zb + 1).wait()
 
         @pl.when(zb >= 2)
         def _():
@@ -461,13 +523,14 @@
         flat = out_buf.reshape(8 * 512, 128)
         for i in range(8):
             gather_z(jnp.minimum(zb * 8 + i + 1, 63), (i + 1) % 2)
-            pre = acc_ref[i % 2, 0:64, :] + bias
+            pre = acc_ref[i % 2, 0:64, :]
             tan = acc_ref[i % 2, 64:128, :]
             sq = pre * pre
             t = jnp.tanh(pre * (c0 + (c0 * 0.044715) * sq))
             half = 0.5 + 0.5 * t
-            slope = half + (0.5 * pre) * ((1.0 - t * t) * (c0 + (3.0 * 0.044715 * c0) * sq))
-            for n, val in enumerate((pre * half, slope * tan)):
+            res = pre * half
+            slope = half + res * ((1.0 - t) * (c0 + (3.0 * 0.044715 * c0) * sq))
+            for n, val in enumerate((res, slope * tan)):
                 for h in range(2):
                     flat[pl.ds(slot * 2048 + n * 1024 + h * 512 + i, 64, stride=8), :] = val[:, h * 128 : (h + 1) * 128]
         for c in copies(zb, slot):
@@ -480,20 +543,20 @@
             c.wait()
 
 
-def inverse(xs, g, pm, zm, lw, bias):
+def inverse(loc, g, v, tz):
     out = jax.ShapeDtypeStruct((64, ZL, FL), F32)
     return pl.pallas_call(
         inverse_kernel,
         out_shape=(out, out),
-        in_specs=[VMEM, VMEM, VMEM, VMEM, VMEM, VMEM],
+        in_specs=[HBM, VMEM, VMEM, VMEM],
         out_specs=(HBM, HBM),
         scratch_shapes=[
-            pltpu.VMEM((8192, 128), F32), pltpu.VMEM((2, 128, FL), F32), pltpu.VMEM((8, 64, 8, 128), F32),
-            pltpu.SemaphoreType.DMA((8,)),
+            pltpu.VMEM((8192, FL), F32), pltpu.VMEM((8192, 128), F32), pltpu.VMEM((2, 128, FL), F32), pltpu.VMEM((8, 64, 8, 128), F32),
+            pltpu.SemaphoreType.DMA((8,)), pltpu.SemaphoreType.DMA((8,)),
         ],
         compiler_params=pltpu.CompilerParams(vmem_limit_bytes=VMEM_INVERSE),
         name="inverse_kernel",
-    )(xs, g, pm, zm, lw, bias)
+    )(loc, g, v, tz)
 
 
 def body(field, field_tangent, spectral_weight, local_weight, bias_term, z_modes, phi_modes):
@@ -506,9 +569,8 @@
     lane_o = lane // 4 % 16
     pick = ((o == lane_o) & (c == (lane_o + d) % 16)).astype(F32)
     wd = jnp.einsum("icokhq,codl->dihkql", w, pick, precision=lax.Precision.HIGHEST).reshape(1024, 128)
-    s, xs = forward(x0, x1, pm, zm)
-    g = exchange(s, wd)
-    out, tan = inverse(xs, g, pm, zm, local_weight, bias_term.reshape(1, 16))
+    g, loc, v, tz = exchange(x0, x1, pm, zm, wd, local_weight, bias_term.reshape(1, 16))
+    out, tan = inverse(loc, g.reshape(8192, 128), v, tz)
     return out.reshape(16, 4, ZL, FL), tan.reshape(16, 4, ZL, FL)
 
 

time: 75.6 us -> 72.8 us (0.963)
  Pallas kernels: 72.4 us -> 69.7 us
    pallas_call x3 -> x2, Pallas kernels: 72.4 us -> 69.7 us  [the longest x1 59.7 us: exchange(): pl.pallas_call(exchange_kernel, out_shape=(jax.ShapeDtypeStruct((2, 4, 8,...]
where the time goes in v1:
time: 72.8 us; the launch traced here: 72.6 us
  Pallas kernels  69.7 us (96%)
  local copies, waits for them, and re-layouts  1.3 us (2%)
  matrix products  0.92 us (1%)
  between operations  0.73 us (1%)
    pallas_call x1, Pallas kernels, exchange(): pl.pallas_call(exchange_kernel, out_shape=(jax.ShapeDtypeStruct((2, 4, 8,...  59.7 us
    pallas_call x1, Pallas kernels, inverse(): pl.pallas_call(inverse_kernel, out_shape=(out, out), in_specs=[HBM, VMEM,...  9.96 us

profile of v1, /device:TPU:1, one launch (start us, length us, event | category | flops | bytes accessed | tf_op | source)
XLA Modules:
  0.0 72.6 jit_solution(15210834965502238568)
XLA Ops:
  0.7 1.2 %copy.11 = f32[2,16,16,2,16]{2,4,3,1,0:T(8,128)S(1)} copy(f32[2,16,16,2,16]{4,3,2,1,0:T(2,128)} %param.9) | data formatting | bytes 131072 | tf_op args[2]
  1.9 0.0 copy-start
  1.9 0.0 copy-start.1
  1.9 0.0 copy-start.2
  1.9 0.0 copy-start.3
  1.9 0.9 %fusion.15 = f32[16,2,2,2,8,128]{5,4,2,3,1,0:T(8,128)S(1)} fusion(s32[128]{0:T(128)S(1)} %get-tuple-element.14, s32[128]{0:T(128)S(1)} %get-tuple-element.15, pred[128]{0:T(512)(128)(4,1)S(1)} %compare_and_fusion, f32[2,16,16,2,16]{2,4,3,1,0:T(8,128)S(1)} %copy.11), kind=kOutput, calls=%fused_computation.21 | convolution fusion | flops 416808960 | bytes 590976 | tf_op jit(solution)/shard_map/icokhq,codl->dihkql/dot_general | solution.py:571
  2.9 0.0 copy-done
  2.9 0.0 copy-done.1
  2.9 0.0 copy-done.2
  2.9 0.0 copy-done.3
  3.0 59.7 %exchange_kernel.1 = (f32[2,4,8,4,32,128]{5,4,3,2,1,0:T(8,128)S(1)}, f32[8192,256]{1,0:T(8,128)}, bf16[256,256]{1,0:T(8,128)(2,1)S(1)}, bf16[128,256]{1,0:T(8,128)(2,1)S(1)}) custom-call(f32[64,64,256]{2,1,0:T(8,128)} %bitcast.33, f32[64,64,256]{2,1,0:T(8,128)} %bitcast.34, s32[1,64]{1,0:T(1,128)S(1)} %bitcast.30, s32[1,64]{1,0:T(1,128)S(1)} %bitcast.31, ...), custom_call_target="tpu_custom_call" | custom-call | tf_op jit(solution)/shard_map/exchange_kernel/pallas_call | solution.py:442
  62.7 10.0 %inverse_kernel.1 = (f32[64,64,256]{2,1,0:T(8,128)}, f32[64,64,256]{2,1,0:T(8,128)}) custom-call(f32[8192,256]{1,0:T(8,128)} %get-tuple-element.8.loc_hbm, f32[8192,128]{1,0:T(8,128)S(1)} %bitcast.28, bf16[256,256]{1,0:T(8,128)(2,1)S(1)} %get-tuple-element.10.v_ref, bf16[128,256]{1,0:T(8,128)(2,1)S(1)} %get-tuple-element.11.tz_ref), custom_call_target="tpu_custom_call" | custom-call | tf_op jit(solution)/shard_map/inverse_kernel/pallas_call | solution.py:548
  (3 shorter events, 0.1 us)
Async XLA Ops:
  1.9 1.0 %copy-start = (f32[16,16]{1,0:T(8,128)S(1)}, f32[16,16]{1,0:T(8,128)}, u32[]{:S(2)}) copy-start(f32[16,16]{1,0:T(8,128)} %lw_ref.1) | copy-start | bytes 3076
  1.9 1.0 %copy-start.1 = (s32[64]{0:T(128)S(1)}, s32[64]{0:T(128)}, u32[]{:S(2)}) copy-start(s32[64]{0:T(128)} %param.13) | copy-start | bytes 772
  1.9 1.0 %copy-start.2 = (s32[64]{0:T(128)S(1)}, s32[64]{0:T(128)}, u32[]{:S(2)}) copy-start(s32[64]{0:T(128)} %param.12) | copy-start | bytes 772
  1.9 1.0 %copy-start.3 = (f32[16]{0:T(128)S(1)}, f32[16]{0:T(128)}, u32[]{:S(2)}) copy-start(f32[16]{0:T(128)} %param.11) | copy-start | bytes 196

commit v2 on v1

--- a/solution.py
+++ b/solution.py
@@ -110,29 +110,25 @@
         for c in fetch(x0_ref, x1_ref, x_buf, sem, zb):
             c.wait()
 
-    arrive(0)
-
-    def block(zb, carry):
-        @pl.when(zb < 7)
-        def _():
-            arrive(zb + 1)
-
-        base = pl.multiple_of(zb * 1024, 1024)
-        base2 = pl.multiple_of(zb * 2048, 2048)
-        for i in range(4):
+    def block(k, carry):
+        for n in range(2):
+            arrive(2 * k + n)
+        for i in range(8):
+            base = pl.multiple_of(k * 2048, 2048) + i // 4 * 1024
+            base2 = pl.multiple_of(k * 4096, 4096) + i * 512
             for n in range(2):
-                hi, lo = split(stack_z(x_buf, zb, i * 2 + n))
-                xs_ref[pl.ds(base2 + (i * 512 + n * 128), 128), :] = hi
-                xs_ref[pl.ds(base2 + (i * 512 + 256 + n * 128), 128), :] = lo
-            hi = xs_ref[pl.ds(base2 + i * 512, 256), :]
-            lo = xs_ref[pl.ds(base2 + (i * 512 + 256), 256), :]
+                hi, lo = split(stack_z(x_buf, 2 * k + i // 4, i % 4 * 2 + n))
+                xs_ref[pl.ds(base2 + n * 128, 128), :] = hi
+                xs_ref[pl.ds(base2 + (256 + n * 128), 128), :] = lo
+            hi = xs_ref[pl.ds(base2, 256), :]
+            lo = xs_ref[pl.ds(base2 + 256, 256), :]
             o = nt(w2, hi)
             o = o[:128] + (o[128:] + nt(w_hi, lo))
             for n in range(2):
-                a_ref[pl.ds(base + (i * 2 + n), 128, stride=8), :] = o[:, n * 128 : (n + 1) * 128]
+                a_ref[pl.ds(base + (i % 4 * 2 + n), 128, stride=8), :] = o[:, n * 128 : (n + 1) * 128]
         return carry
 
-    lax.fori_loop(0, 8, block, 0)
+    lax.fori_loop(0, 4, block, 0)
 
     def pair(j, carry):
         base = pl.multiple_of(((j // 4) * 16 + j % 4 * 2) * 8, 16)
@@ -150,7 +146,7 @@
                 s_ref[spots[n][g], :] = o[g * 8 : g * 8 + 8, n * 128 : (n + 1) * 128]
         return carry
 
-    lax.fori_loop(0, 32, pair, 0, unroll=8)
+    lax.fori_loop(0, 32, pair, 0, unroll=16)
 
 
 def inverse_z(modes_ref, t_ref):
@@ -288,7 +284,6 @@
         stores.append(c)
 
     mix_local(0)
-    mix_local(1)
 
     def land(n):
         pairs[n].wait_recv()
@@ -304,7 +299,7 @@
         n = s * 6
         relays[0, s] = send(piece(0, s, 0), relay.at[0, s], st1_s.at[n], st1_r.at[n], right)
         relays[1, s] = send(piece(0, s, 1), relay.at[1, s], st1_s.at[n + 1], st1_r.at[n + 1], left)
-    mix_local(2)
+    mix_local(1)
     land(1)
     land(2)
     first = {}
@@ -314,7 +309,7 @@
             send(piece(1, s, 1), fin.at[0, s, pl.ds(4, 4)], st1_s.at[n + 2], st1_r.at[n + 2], right),
             send(piece(2, s, 0), fin.at[1, s, pl.ds(0, 4)], st1_s.at[n + 3], st1_r.at[n + 3], left),
         ]
-        mix_local(3 + turns.index(s))
+        mix_local(2 + turns.index(s))
         for side, dev in enumerate((right, left)):
             relays[side, s].wait_recv()
             ref = piece(1 + side, s, side)
@@ -339,7 +334,7 @@
             part = second.at[s, pl.ds(h * 4, 4)]
             part[...] = part[...] + relay2[h]
             sends2.append(send(second.at[s], rec2.at[h], st2_s.at[2 + h], st2_r.at[2 + h], along_b(s)))
-    mix_local(7)
+    mix_local(6)
     for c in sends2:
         c.wait_recv()
     third[...] = (second[0] + (rec2[0] + rec2[1])).reshape(4, 64, 128)
@@ -347,6 +342,7 @@
     sends3 = []
     for t in turns[:3]:
         sends3.append(send(third.at[(pd + t) % 4], rec3.at[t - 1], st3_s.at[t - 1], st3_r.at[t - 1], along_d(t)))
+    mix_local(7)
     for c in sends3:
         c.wait_recv()
     own[...] = third[pd] + rec3[0] + (rec3[1] + rec3[2])
@@ -483,7 +479,7 @@
                 u_ref[pl.ds(base + (n + g * 64), 8, stride=8), :] = o[g * 8 : g * 8 + 8, n * 128 : (n + 1) * 128]
         return carry
 
-    lax.fori_loop(0, 32, pair, 0, unroll=8)
+    lax.fori_loop(0, 32, pair, 0, unroll=16)
     v_hi, v_lo = v_ref[0:128, :], v_ref[128:256, :]
     v3 = cat([v_hi, v_hi, v_lo], 0)
     c0 = math.sqrt(2.0 / math.pi)
@@ -508,36 +504,39 @@
     take(0).wait()
     gather_z(0, 0)
 
-    def block(zb, carry):
-        slot = zb % 2
-
-        @pl.when(zb < 7)
+    def block(k, carry):
+        take(2 * k + 1).wait()
+
+        @pl.when(k < 3)
         def _():
-            take(zb + 1).wait()
-
-        @pl.when(zb >= 2)
+            take(2 * k + 2).wait()
+
+        @pl.when(k >= 1)
         def _():
+            for n in range(2):
+                for c in copies(2 * k + n, n):
+                    c.wait()
+
+        flat = out_buf.reshape(8 * 512, 128)
+        for slot in range(2):
+            zb = 2 * k + slot
+            for i in range(8):
+                gather_z(jnp.minimum(zb * 8 + i + 1, 63), (i + 1) % 2)
+                pre = acc_ref[i % 2, 0:64, :]
+                tan = acc_ref[i % 2, 64:128, :]
+                sq = pre * pre
+                t = jnp.tanh(pre * (c0 + (c0 * 0.044715) * sq))
+                half = 0.5 + 0.5 * t
+                res = pre * half
+                slope = half + res * ((1.0 - t) * (c0 + (3.0 * 0.044715 * c0) * sq))
+                for n, val in enumerate((res, slope * tan)):
+                    for h in range(2):
+                        flat[pl.ds(slot * 2048 + n * 1024 + h * 512 + i, 64, stride=8), :] = val[:, h * 128 : (h + 1) * 128]
             for c in copies(zb, slot):
-                c.wait()
-
-        flat = out_buf.reshape(8 * 512, 128)
-        for i in range(8):
-            gather_z(jnp.minimum(zb * 8 + i + 1, 63), (i + 1) % 2)
-            pre = acc_ref[i % 2, 0:64, :]
-            tan = acc_ref[i % 2, 64:128, :]
-            sq = pre * pre
-            t = jnp.tanh(pre * (c0 + (c0 * 0.044715) * sq))
-            half = 0.5 + 0.5 * t
-            res = pre * half
-            slope = half + res * ((1.0 - t) * (c0 + (3.0 * 0.044715 * c0) * sq))
-            for n, val in enumerate((res, slope * tan)):
-                for h in range(2):
-                    flat[pl.ds(slot * 2048 + n * 1024 + h * 512 + i, 64, stride=8), :] = val[:, h * 128 : (h + 1) * 128]
-        for c in copies(zb, slot):
-            c.start()
+                c.start()
         return carry
 
-    lax.fori_loop(0, 8, block, 0)
+    lax.fori_loop(0, 4, block, 0)
     for zb in (6, 7):
         for c in copies(zb, zb % 2):
             c.wait()

time: 72.8 us -> 72.7 us (level)
    pallas_call x1, Pallas kernels: 59.7 us -> 58.1 us  [exchange(): pl.pallas_call(exchange_kernel, out_shape=(jax.ShapeDtypeStruct((2, 4, 8,...]
    pallas_call x1, Pallas kernels: 9.96 us -> 11.5 us  [inverse(): pl.pallas_call(inverse_kernel, out_shape=(out, out), in_specs=[HBM, VMEM,...]
where the time goes in v2:
time: 72.7 us; the launch traced here: 72.6 us
  Pallas kernels  69.6 us (96%)
  local copies, waits for them, and re-layouts  1.3 us (2%)
  matrix products  0.92 us (1%)
  between operations  0.73 us (1%)
    pallas_call x1, Pallas kernels, exchange(): pl.pallas_call(exchange_kernel, out_shape=(jax.ShapeDtypeStruct((2, 4, 8,...  58.1 us
    pallas_call x1, Pallas kernels, inverse(): pl.pallas_call(inverse_kernel, out_shape=(out, out), in_specs=[HBM, VMEM,...  11.5 us

profile of v2, /device:TPU:1, one launch (start us, length us, event | category | flops | bytes accessed | tf_op | source)
XLA Modules:
  0.0 72.6 jit_solution(17706970853664914578)
XLA Ops:
  0.7 1.2 %copy.11 = f32[2,16,16,2,16]{2,4,3,1,0:T(8,128)S(1)} copy(f32[2,16,16,2,16]{4,3,2,1,0:T(2,128)} %param.9) | data formatting | bytes 131072 | tf_op args[2]
  1.9 0.0 copy-start
  1.9 0.0 copy-start.1
  1.9 0.0 copy-start.2
  1.9 0.0 copy-start.3
  1.9 0.9 %fusion.15 = f32[16,2,2,2,8,128]{5,4,2,3,1,0:T(8,128)S(1)} fusion(s32[128]{0:T(128)S(1)} %get-tuple-element.14, s32[128]{0:T(128)S(1)} %get-tuple-element.15, pred[128]{0:T(512)(128)(4,1)S(1)} %compare_and_fusion, f32[2,16,16,2,16]{2,4,3,1,0:T(8,128)S(1)} %copy.11), kind=kOutput, calls=%fused_computation.21 | convolution fusion | flops 416808960 | bytes 590976 | tf_op jit(solution)/shard_map/icokhq,codl->dihkql/dot_general | solution.py:570
  2.9 0.0 copy-done
  2.9 0.0 copy-done.1
  2.9 0.0 copy-done.2
  2.9 0.0 copy-done.3
  3.0 58.1 %exchange_kernel.1 = (f32[2,4,8,4,32,128]{5,4,3,2,1,0:T(8,128)S(1)}, f32[8192,256]{1,0:T(8,128)}, bf16[256,256]{1,0:T(8,128)(2,1)S(1)}, bf16[128,256]{1,0:T(8,128)(2,1)S(1)}) custom-call(f32[64,64,256]{2,1,0:T(8,128)} %bitcast.33, f32[64,64,256]{2,1,0:T(8,128)} %bitcast.34, s32[1,64]{1,0:T(1,128)S(1)} %bitcast.30, s32[1,64]{1,0:T(1,128)S(1)} %bitcast.31, ...), custom_call_target="tpu_custom_call" | custom-call | tf_op jit(solution)/shard_map/exchange_kernel/pallas_call | solution.py:438
  61.1 11.5 %inverse_kernel.1 = (f32[64,64,256]{2,1,0:T(8,128)}, f32[64,64,256]{2,1,0:T(8,128)}) custom-call(f32[8192,256]{1,0:T(8,128)} %get-tuple-element.8.loc_hbm, f32[8192,128]{1,0:T(8,128)S(1)} %bitcast.28, bf16[256,256]{1,0:T(8,128)(2,1)S(1)} %get-tuple-element.10.v_ref, bf16[128,256]{1,0:T(8,128)(2,1)S(1)} %get-tuple-element.11.tz_ref), custom_call_target="tpu_custom_call" | custom-call | tf_op jit(solution)/shard_map/inverse_kernel/pallas_call | solution.py:547
  (3 shorter events, 0.1 us)
Async XLA Ops:
  1.9 1.0 %copy-start = (f32[16,16]{1,0:T(8,128)S(1)}, f32[16,16]{1,0:T(8,128)}, u32[]{:S(2)}) copy-start(f32[16,16]{1,0:T(8,128)} %lw_ref.1) | copy-start | bytes 3076
  1.9 1.0 %copy-start.1 = (s32[64]{0:T(128)S(1)}, s32[64]{0:T(128)}, u32[]{:S(2)}) copy-start(s32[64]{0:T(128)} %param.13) | copy-start | bytes 772
  1.9 1.0 %copy-start.2 = (s32[64]{0:T(128)S(1)}, s32[64]{0:T(128)}, u32[]{:S(2)}) copy-start(s32[64]{0:T(128)} %param.12) | copy-start | bytes 772
  1.9 1.0 %copy-start.3 = (f32[16]{0:T(128)S(1)}, f32[16]{0:T(128)}, u32[]{:S(2)}) copy-start(f32[16]{0:T(128)} %param.11) | copy-start | bytes 196

commit v3 on v1

--- a/solution.py
+++ b/solution.py
@@ -110,29 +110,25 @@
         for c in fetch(x0_ref, x1_ref, x_buf, sem, zb):
             c.wait()
 
-    arrive(0)
-
-    def block(zb, carry):
-        @pl.when(zb < 7)
-        def _():
-            arrive(zb + 1)
-
-        base = pl.multiple_of(zb * 1024, 1024)
-        base2 = pl.multiple_of(zb * 2048, 2048)
-        for i in range(4):
+    def block(k, carry):
+        for n in range(2):
+            arrive(2 * k + n)
+        for i in range(8):
+            base = pl.multiple_of(k * 2048, 2048) + i // 4 * 1024
+            base2 = pl.multiple_of(k * 4096, 4096) + i * 512
             for n in range(2):
-                hi, lo = split(stack_z(x_buf, zb, i * 2 + n))
-                xs_ref[pl.ds(base2 + (i * 512 + n * 128), 128), :] = hi
-                xs_ref[pl.ds(base2 + (i * 512 + 256 + n * 128), 128), :] = lo
-            hi = xs_ref[pl.ds(base2 + i * 512, 256), :]
-            lo = xs_ref[pl.ds(base2 + (i * 512 + 256), 256), :]
+                hi, lo = split(stack_z(x_buf, 2 * k + i // 4, i % 4 * 2 + n))
+                xs_ref[pl.ds(base2 + n * 128, 128), :] = hi
+                xs_ref[pl.ds(base2 + (256 + n * 128), 128), :] = lo
+            hi = xs_ref[pl.ds(base2, 256), :]
+            lo = xs_ref[pl.ds(base2 + 256, 256), :]
             o = nt(w2, hi)
             o = o[:128] + (o[128:] + nt(w_hi, lo))
             for n in range(2):
-                a_ref[pl.ds(base + (i * 2 + n), 128, stride=8), :] = o[:, n * 128 : (n + 1) * 128]
+                a_ref[pl.ds(base + (i % 4 * 2 + n), 128, stride=8), :] = o[:, n * 128 : (n + 1) * 128]
         return carry
 
-    lax.fori_loop(0, 8, block, 0)
+    lax.fori_loop(0, 4, block, 0)
 
     def pair(j, carry):
         base = pl.multiple_of(((j // 4) * 16 + j % 4 * 2) * 8, 16)
@@ -150,7 +146,7 @@
                 s_ref[spots[n][g], :] = o[g * 8 : g * 8 + 8, n * 128 : (n + 1) * 128]
         return carry
 
-    lax.fori_loop(0, 32, pair, 0, unroll=8)
+    lax.fori_loop(0, 32, pair, 0, unroll=16)
 
 
 def inverse_z(modes_ref, t_ref):
@@ -288,7 +284,6 @@
         stores.append(c)
 
     mix_local(0)
-    mix_local(1)
 
     def land(n):
         pairs[n].wait_recv()
@@ -304,7 +299,7 @@
         n = s * 6
         relays[0, s] = send(piece(0, s, 0), relay.at[0, s], st1_s.at[n], st1_r.at[n], right)
         relays[1, s] = send(piece(0, s, 1), relay.at[1, s], st1_s.at[n + 1], st1_r.at[n + 1], left)
-    mix_local(2)
+    mix_local(1)
     land(1)
     land(2)
     first = {}
@@ -314,7 +309,7 @@
             send(piece(1, s, 1), fin.at[0, s, pl.ds(4, 4)], st1_s.at[n + 2], st1_r.at[n + 2], right),
             send(piece(2, s, 0), fin.at[1, s, pl.ds(0, 4)], st1_s.at[n + 3], st1_r.at[n + 3], left),
         ]
-        mix_local(3 + turns.index(s))
+        mix_local(2 + turns.index(s))
         for side, dev in enumerate((right, left)):
             relays[side, s].wait_recv()
             ref = piece(1 + side, s, side)
@@ -339,7 +334,7 @@
             part = second.at[s, pl.ds(h * 4, 4)]
             part[...] = part[...] + relay2[h]
             sends2.append(send(second.at[s], rec2.at[h], st2_s.at[2 + h], st2_r.at[2 + h], along_b(s)))
-    mix_local(7)
+    mix_local(6)
     for c in sends2:
         c.wait_recv()
     third[...] = (second[0] + (rec2[0] + rec2[1])).reshape(4, 64, 128)
@@ -347,6 +342,7 @@
     sends3 = []
     for t in turns[:3]:
         sends3.append(send(third.at[(pd + t) % 4], rec3.at[t - 1], st3_s.at[t - 1], st3_r.at[t - 1], along_d(t)))
+    mix_local(7)
     for c in sends3:
         c.wait_recv()
     own[...] = third[pd] + rec3[0] + (rec3[1] + rec3[2])
@@ -483,7 +479,7 @@
                 u_ref[pl.ds(base + (n + g * 64), 8, stride=8), :] = o[g * 8 : g * 8 + 8, n * 128 : (n + 1) * 128]
         return carry
 
-    lax.fori_loop(0, 32, pair, 0, unroll=8)
+    lax.fori_loop(0, 32, pair, 0, unroll=16)
     v_hi, v_lo = v_ref[0:128, :], v_ref[128:256, :]
     v3 = cat([v_hi, v_hi, v_lo], 0)
     c0 = math.sqrt(2.0 / math.pi)

time: 72.8 us -> 71.2 us (0.978)
  Pallas kernels: 69.7 us -> 68 us
    pallas_call x1, Pallas kernels: 59.7 us -> 58.1 us  [exchange(): pl.pallas_call(exchange_kernel, out_shape=(jax.ShapeDtypeStruct((2, 4, 8,...]
where the time goes in v3:
time: 71.2 us; the launch traced here: 71 us
  Pallas kernels  68 us (96%)
  local copies, waits for them, and re-layouts  1.3 us (2%)
  matrix products  0.92 us (1%)
  between operations  0.73 us (1%)
    pallas_call x1, Pallas kernels, exchange(): pl.pallas_call(exchange_kernel, out_shape=(jax.ShapeDtypeStruct((2, 4, 8,...  58.1 us
    pallas_call x1, Pallas kernels, inverse(): pl.pallas_call(inverse_kernel, out_shape=(out, out), in_specs=[HBM, VMEM,...  9.91 us

profile of v3, /device:TPU:1, one launch (start us, length us, event | category | flops | bytes accessed | tf_op | source)
XLA Modules:
  0.0 71.0 jit_solution(7007082781532267456)
XLA Ops:
  0.7 1.2 %copy.11 = f32[2,16,16,2,16]{2,4,3,1,0:T(8,128)S(1)} copy(f32[2,16,16,2,16]{4,3,2,1,0:T(2,128)} %param.9) | data formatting | bytes 131072 | tf_op args[2]
  1.9 0.0 copy-start
  1.9 0.0 copy-start.1
  1.9 0.0 copy-start.2
  1.9 0.0 copy-start.3
  1.9 0.9 %fusion.15 = f32[16,2,2,2,8,128]{5,4,2,3,1,0:T(8,128)S(1)} fusion(s32[128]{0:T(128)S(1)} %get-tuple-element.14, s32[128]{0:T(128)S(1)} %get-tuple-element.15, pred[128]{0:T(512)(128)(4,1)S(1)} %compare_and_fusion, f32[2,16,16,2,16]{2,4,3,1,0:T(8,128)S(1)} %copy.11), kind=kOutput, calls=%fused_computation.21 | convolution fusion | flops 416808960 | bytes 590976 | tf_op jit(solution)/shard_map/icokhq,codl->dihkql/dot_general | solution.py:567
  2.9 0.0 copy-done
  2.9 0.0 copy-done.1
  2.9 0.0 copy-done.2
  2.9 0.0 copy-done.3
  3.0 58.1 %exchange_kernel.1 = (f32[2,4,8,4,32,128]{5,4,3,2,1,0:T(8,128)S(1)}, f32[8192,256]{1,0:T(8,128)}, bf16[256,256]{1,0:T(8,128)(2,1)S(1)}, bf16[128,256]{1,0:T(8,128)(2,1)S(1)}) custom-call(f32[64,64,256]{2,1,0:T(8,128)} %bitcast.33, f32[64,64,256]{2,1,0:T(8,128)} %bitcast.34, s32[1,64]{1,0:T(1,128)S(1)} %bitcast.30, s32[1,64]{1,0:T(1,128)S(1)} %bitcast.31, ...), custom_call_target="tpu_custom_call" | custom-call | tf_op jit(solution)/shard_map/exchange_kernel/pallas_call | solution.py:438
  61.1 9.9 %inverse_kernel.1 = (f32[64,64,256]{2,1,0:T(8,128)}, f32[64,64,256]{2,1,0:T(8,128)}) custom-call(f32[8192,256]{1,0:T(8,128)} %get-tuple-element.8.loc_hbm, f32[8192,128]{1,0:T(8,128)S(1)} %bitcast.28, bf16[256,256]{1,0:T(8,128)(2,1)S(1)} %get-tuple-element.10.v_ref, bf16[128,256]{1,0:T(8,128)(2,1)S(1)} %get-tuple-element.11.tz_ref), custom_call_target="tpu_custom_call" | custom-call | tf_op jit(solution)/shard_map/inverse_kernel/pallas_call | solution.py:544
  (3 shorter events, 0.1 us)
Async XLA Ops:
  1.9 1.0 %copy-start = (f32[16,16]{1,0:T(8,128)S(1)}, f32[16,16]{1,0:T(8,128)}, u32[]{:S(2)}) copy-start(f32[16,16]{1,0:T(8,128)} %lw_ref.1) | copy-start | bytes 3076
  1.9 1.0 %copy-start.1 = (s32[64]{0:T(128)S(1)}, s32[64]{0:T(128)}, u32[]{:S(2)}) copy-start(s32[64]{0:T(128)} %param.13) | copy-start | bytes 772
  1.9 1.0 %copy-start.2 = (s32[64]{0:T(128)S(1)}, s32[64]{0:T(128)}, u32[]{:S(2)}) copy-start(s32[64]{0:T(128)} %param.12) | copy-start | bytes 772
  1.9 1.0 %copy-start.3 = (f32[16]{0:T(128)S(1)}, f32[16]{0:T(128)}, u32[]{:S(2)}) copy-start(f32[16]{0:T(128)} %param.11) | copy-start | bytes 196

commit v4 on v2

--- a/solution.py
+++ b/solution.py
@@ -511,15 +511,16 @@
         def _():
             take(2 * k + 2).wait()
 
-        @pl.when(k >= 1)
+        @pl.when(k >= 2)
         def _():
             for n in range(2):
-                for c in copies(2 * k + n, n):
+                for c in copies(2 * k + n, k % 2 * 2 + n):
                     c.wait()
 
-        flat = out_buf.reshape(8 * 512, 128)
-        for slot in range(2):
-            zb = 2 * k + slot
+        flat = out_buf.reshape(16 * 512, 128)
+        for n2 in range(2):
+            zb = 2 * k + n2
+            slot = k % 2 * 2 + n2
             for i in range(8):
                 gather_z(jnp.minimum(zb * 8 + i + 1, 63), (i + 1) % 2)
                 pre = acc_ref[i % 2, 0:64, :]
@@ -537,8 +538,8 @@
         return carry
 
     lax.fori_loop(0, 4, block, 0)
-    for zb in (6, 7):
-        for c in copies(zb, zb % 2):
+    for zb in (4, 5, 6, 7):
+        for c in copies(zb, zb % 4):
             c.wait()
 
 
@@ -550,8 +551,8 @@
         in_specs=[HBM, VMEM, VMEM, VMEM],
         out_specs=(HBM, HBM),
         scratch_shapes=[
-            pltpu.VMEM((8192, FL), F32), pltpu.VMEM((8192, 128), F32), pltpu.VMEM((2, 128, FL), F32), pltpu.VMEM((8, 64, 8, 128), F32),
-            pltpu.SemaphoreType.DMA((8,)), pltpu.SemaphoreType.DMA((8,)),
+            pltpu.VMEM((8192, FL), F32), pltpu.VMEM((8192, 128), F32), pltpu.VMEM((2, 128, FL), F32), pltpu.VMEM((16, 64, 8, 128), F32),
+            pltpu.SemaphoreType.DMA((8,)), pltpu.SemaphoreType.DMA((16,)),
         ],
         compiler_params=pltpu.CompilerParams(vmem_limit_bytes=VMEM_INVERSE),
         name="inverse_kernel",

time: 72.7 us -> 70 us (0.963)
  Pallas kernels: 69.6 us -> 66.8 us
    pallas_call x1, Pallas kernels: 11.5 us -> 8.71 us  [inverse(): pl.pallas_call(inverse_kernel, out_shape=(out, out), in_specs=[HBM, VMEM,...]
where the time goes in v4:
time: 70 us; the launch traced here: 69.8 us
  Pallas kernels  66.8 us (95%)
  local copies, waits for them, and re-layouts  1.3 us (2%)
  matrix products  0.92 us (1%)
  between operations  0.73 us (1%)
    pallas_call x1, Pallas kernels, exchange(): pl.pallas_call(exchange_kernel, out_shape=(jax.ShapeDtypeStruct((2, 4, 8,...  58.1 us
    pallas_call x1, Pallas kernels, inverse(): pl.pallas_call(inverse_kernel, out_shape=(out, out), in_specs=[HBM, VMEM,...  8.71 us

profile of v4, /device:TPU:1, one launch (start us, length us, event | category | flops | bytes accessed | tf_op | source)
XLA Modules:
  0.0 69.8 jit_solution(2512805135285066247)
XLA Ops:
  0.7 1.2 %copy.11 = f32[2,16,16,2,16]{2,4,3,1,0:T(8,128)S(1)} copy(f32[2,16,16,2,16]{4,3,2,1,0:T(2,128)} %param.9) | data formatting | bytes 131072 | tf_op args[2]
  1.9 0.0 copy-start
  1.9 0.0 copy-start.1
  1.9 0.0 copy-start.2
  1.9 0.0 copy-start.3
  1.9 0.9 %fusion.15 = f32[16,2,2,2,8,128]{5,4,2,3,1,0:T(8,128)S(1)} fusion(s32[128]{0:T(128)S(1)} %get-tuple-element.14, s32[128]{0:T(128)S(1)} %get-tuple-element.15, pred[128]{0:T(512)(128)(4,1)S(1)} %compare_and_fusion, f32[2,16,16,2,16]{2,4,3,1,0:T(8,128)S(1)} %copy.11), kind=kOutput, calls=%fused_computation.21 | convolution fusion | flops 416808960 | bytes 590976 | tf_op jit(solution)/shard_map/icokhq,codl->dihkql/dot_general | solution.py:571
  2.9 0.0 copy-done
  2.9 0.0 copy-done.1
  2.9 0.0 copy-done.2
  2.9 0.0 copy-done.3
  3.0 58.1 %exchange_kernel.1 = (f32[2,4,8,4,32,128]{5,4,3,2,1,0:T(8,128)S(1)}, f32[8192,256]{1,0:T(8,128)}, bf16[256,256]{1,0:T(8,128)(2,1)S(1)}, bf16[128,256]{1,0:T(8,128)(2,1)S(1)}) custom-call(f32[64,64,256]{2,1,0:T(8,128)} %bitcast.33, f32[64,64,256]{2,1,0:T(8,128)} %bitcast.34, s32[1,64]{1,0:T(1,128)S(1)} %bitcast.30, s32[1,64]{1,0:T(1,128)S(1)} %bitcast.31, ...), custom_call_target="tpu_custom_call" | custom-call | tf_op jit(solution)/shard_map/exchange_kernel/pallas_call | solution.py:438
  61.1 8.7 %inverse_kernel.1 = (f32[64,64,256]{2,1,0:T(8,128)}, f32[64,64,256]{2,1,0:T(8,128)}) custom-call(f32[8192,256]{1,0:T(8,128)} %get-tuple-element.8.loc_hbm, f32[8192,128]{1,0:T(8,128)S(1)} %bitcast.28, bf16[256,256]{1,0:T(8,128)(2,1)S(1)} %get-tuple-element.10.v_ref, bf16[128,256]{1,0:T(8,128)(2,1)S(1)} %get-tuple-element.11.tz_ref), custom_call_target="tpu_custom_call" | custom-call | tf_op jit(solution)/shard_map/inverse_kernel/pallas_call | solution.py:548
  (3 shorter events, 0.1 us)
Async XLA Ops:
  1.9 1.0 %copy-start = (f32[16,16]{1,0:T(8,128)S(1)}, f32[16,16]{1,0:T(8,128)}, u32[]{:S(2)}) copy-start(f32[16,16]{1,0:T(8,128)} %lw_ref.1) | copy-start | bytes 3076
  1.9 1.0 %copy-start.1 = (s32[64]{0:T(128)S(1)}, s32[64]{0:T(128)}, u32[]{:S(2)}) copy-start(s32[64]{0:T(128)} %param.13) | copy-start | bytes 772
  1.9 1.0 %copy-start.2 = (s32[64]{0:T(128)S(1)}, s32[64]{0:T(128)}, u32[]{:S(2)}) copy-start(s32[64]{0:T(128)} %param.12) | copy-start | bytes 772
  1.9 1.0 %copy-start.3 = (f32[16]{0:T(128)S(1)}, f32[16]{0:T(128)}, u32[]{:S(2)}) copy-start(f32[16]{0:T(128)} %param.11) | copy-start | bytes 196
